TPU v7x, 32 devices: a whole 2x2x4 slice. The times are simulated.
32 devices in a mesh: row: 4 (over z), col: 4 (over y, x), depth: 2 (over core).
Axes of the slice: x: 2, y: 2, z: 4, core: 2. Of those that a mesh axis runs over, the one named last changes fastest.
Arguments:
- tiles: float32 [4, 4, 96, 256, 256], P('row', 'col', 'depth'), as said below
- tile_rows: int32 [4, 4, 96], P('row', 'col', 'depth'), may hold values from 0 to 127, as said below
- tile_cols: int32 [4, 4, 96], P('row', 'col', 'depth'), may hold values from 0 to 127
- tile_count: int32 [4, 4, 2], P('row', 'col', 'depth'), may hold values from 16 to 48, as said below
Outputs:
- row_scale: float32 [131072], P('row')
- col_scale: float32 [131072], P('col')
- scaled_tiles: float32 [4, 4, 96, 256, 256], P('row', 'col', 'depth')
Inputs may be any that keep to these rules, and one draw needn't show every extreme that they name: `tile_rows`: every block row and every block column of the matrix holds a live tile; no block is listed twice among the live tiles of the two depth lists of one row and col index. `tile_count`: some device's list is full in every draw. `tiles`: entries in empty slots are ignored.
All inputs are finite; a program needn't handle non-finite values.
Results may differ from a plain program's by a relative error of at most 0.0001.
Values sent between devices are 32-bit elements; how exact they have to be, the bound alone decides.
A program may use at most 128 MiB of HBM per device.

v0:
```python
import math
import jax
import jax.numpy as jnp
from jax import lax
from jax.sharding import PartitionSpec as P

RB_DEV = 128
ANCHORS = 16
SWEEPS = 4
EPS = 1e-06


def shards(tiles, tile_rows, tile_cols, tile_count):
    all_values = tiles[0, 0]
    row_index = tile_rows[0, 0]
    col_index = tile_cols[0, 0]
    live_count = tile_count[0, 0, 0]
    slot_count = all_values.shape[0]
    tile_size = all_values.shape[1]
    col_blocks = lax.axis_size("row") * lax.axis_size("depth") * ANCHORS
    group_size = math.gcd(slot_count, 8)
    block_count = (live_count + group_size - 1) // group_size
    row_ids = jnp.arange(RB_DEV, dtype=jnp.int32)
    col_ids = jnp.arange(col_blocks, dtype=jnp.int32)

    def partials(row_now, col_now, summed):

        def step_block(position, carry):
            row_acc, col_acc = carry
            first_slot = position * group_size
            block_values = lax.dynamic_slice_in_dim(all_values, first_slot, group_size, 0)
            block_rows = lax.dynamic_slice_in_dim(row_index, first_slot, group_size, 0)
            block_cols = lax.dynamic_slice_in_dim(col_index, first_slot, group_size, 0)
            live_mask = first_slot + jnp.arange(group_size, dtype=jnp.int32) < live_count
            scaled = (
                block_values * row_now[block_rows][:, :, None] * col_now[block_cols][:, None, :]
            )
            magnitude = jnp.where(live_mask[:, None, None], jnp.abs(scaled), jnp.float32(0.0))
            row_hit = row_ids[:, None] == block_rows[None, :]
            col_hit = col_ids[:, None] == block_cols[None, :]
            if summed:
                row_acc = row_acc + jnp.dot(
                    row_hit.astype(jnp.float32),
                    magnitude.sum(axis=2),
                    precision=lax.Precision.HIGHEST,
                )
                col_acc = col_acc + jnp.dot(
                    col_hit.astype(jnp.float32),
                    magnitude.sum(axis=1),
                    precision=lax.Precision.HIGHEST,
                )
            else:
                row_acc = jnp.maximum(
                    row_acc,
                    jnp.where(
                        row_hit[:, :, None], magnitude.max(axis=2)[None], jnp.float32(0.0)
                    ).max(axis=1),
                )
                col_acc = jnp.maximum(
                    col_acc,
                    jnp.where(
                        col_hit[:, :, None], magnitude.max(axis=1)[None], jnp.float32(0.0)
                    ).max(axis=1),
                )
            return (row_acc, col_acc)

        initial = (
            jnp.zeros((RB_DEV, tile_size), jnp.float32),
            jnp.zeros((col_blocks, tile_size), jnp.float32),
        )
        return lax.fori_loop(0, block_count, step_block, initial)

    row_factor = jnp.ones((RB_DEV, tile_size), jnp.float32)
    col_factor = jnp.ones((col_blocks, tile_size), jnp.float32)
    for sweep_index in range(SWEEPS):
        row_part, col_part = partials(row_factor, col_factor, False)
        row_pair, col_pair = lax.pmax((row_part, col_part), "depth")
        row_peak = lax.pmax(row_pair, "col")
        col_peak = lax.pmax(col_pair, "row")
        row_factor = row_factor * lax.rsqrt(row_peak + EPS)
        col_factor = col_factor * lax.rsqrt(col_peak + EPS)
    row_part, col_part = partials(row_factor, col_factor, True)
    row_mass = lax.psum(row_part, ("col", "depth"))
    col_mass = lax.psum(col_part, ("row", "depth"))
    row_factor = row_factor * lax.rsqrt(row_mass + EPS)
    col_factor = col_factor * lax.rsqrt(col_mass + EPS)
    live_all = jnp.arange(slot_count, dtype=jnp.int32) < live_count
    scaled_all = all_values * row_factor[row_index][:, :, None] * col_factor[col_index][:, None, :]
    scaled_all = jnp.where(live_all[:, None, None], scaled_all, jnp.float32(0.0))
    return (row_factor.reshape(-1), col_factor.reshape(-1), scaled_all[None, None])


def solution(mesh):
    in_specs = (
        P("row", "col", "depth", None, None),
        P("row", "col", "depth"),
        P("row", "col", "depth"),
        P("row", "col", "depth"),
    )
    out_specs = (P("row"), P("col"), P("row", "col", "depth", None, None))
    return jax.shard_map(shards, mesh=mesh, in_specs=in_specs, out_specs=out_specs, check_vma=False)
```

profile of v0, /device:TPU:0, one launch (start us, length us, event | category | flops | bytes accessed | tf_op | source)
XLA Modules:
  0.0 722.1 jit_solution(14367923665303358585)
XLA Ops:
  7.9 17.5 %while.75 = (s32[]{:T(128)}, f32[128,256]{1,0:T(8,128)S(1)}, f32[128,256]{1,0:T(8,128)S(1)}, s32[]{:T(128)}, s32[48]{0:T(128)}, /*index=5*/s32[]{:T(128)}, f32[4...) while((s32[]{:T(128)}, f32[128,256]{1,0:T(8,128)S(1)}, ...), condition=%wide.region_5.6_spmd.clone.clone, body=%wide.region_0.5_spmd.clone.clone.sunk | while | flops 4194374 | bytes 3371599 | solution.py:71
  8.6 0.8 compare_select_fusion.17
  10.6 2.3 fusion.33
  14.4 0.8 compare_select_fusion.17
  16.4 2.3 fusion.33
  20.3 0.8 compare_select_fusion.17
  22.3 2.3 fusion.33
  26.2 37.1 %all-reduce.45.cloned.1.call-done = (f32[128,256]{1,0:T(8,128)}, f32[128,256]{1,0:T(8,128)}) async-done(((f32[128,256]{1,0:T(8,128)}, f32[128,256]{1,0:T(8,128)}), (f32[128,256]{1,0:T(8,128)}, f32[128,256]{1,0:T(8,128)})) %all-reduce.45.cloned.1.call-update) | async-done | bytes 262160 | tf_op jit(solution)/shard_map/pmax | solution.py:77
  63.4 0.7 all-reduce.19.cloned.1.call-update
  64.2 37.4 %all-reduce.21.cloned.1.call-done = f32[128,256]{1,0:T(8,128)} async-done(((f32[128,256]{1,0:T(8,128)}), f32[128,256]{1,0:T(8,128)}) %all-reduce.21.cloned.1.call-update) | async-done | bytes 131088 | tf_op jit(solution)/shard_map/pmax | solution.py:79
  101.6 0.9 add_rsqrt_fusion
  102.5 44.0 %all-reduce.19.cloned.1.call-done = f32[128,256]{1,0:T(8,128)} async-done(((f32[128,256]{1,0:T(8,128)}), f32[128,256]{1,0:T(8,128)}) %all-reduce.19.cloned.1.call-update) | async-done | bytes 131088 | tf_op jit(solution)/shard_map/pmax | solution.py:78
  146.5 0.9 add_rsqrt_fusion.1
  147.5 17.5 %while.76 = (s32[]{:T(128)}, f32[128,256]{1,0:T(8,128)S(1)}, f32[128,256]{1,0:T(8,128)S(1)}, s32[]{:T(128)}, s32[48]{0:T(128)}, /*index=5*/s32[]{:T(128)}, f32[4...) while((s32[]{:T(128)}, f32[128,256]{1,0:T(8,128)S(1)}, ...), condition=%wide.region_15.16_spmd.clone.clone, body=%wide.region_10.15_spmd.clone.clone.sunk | while | flops 4194374 | bytes 3240531 | solution.py:71
  147.5 0.7 add_compare_fusion.11
  148.3 0.8 compare_select_fusion.18
  150.2 2.3 fusion.34
  154.1 0.8 compare_select_fusion.18
  156.0 2.3 fusion.34
  159.9 0.8 compare_select_fusion.18
  161.8 2.3 fusion.34
  165.8 34.9 %all-reduce.43.cloned.1.call-done = (f32[128,256]{1,0:T(8,128)}, f32[128,256]{1,0:T(8,128)}) async-done(((f32[128,256]{1,0:T(8,128)}, f32[128,256]{1,0:T(8,128)}), (f32[128,256]{1,0:T(8,128)}, f32[128,256]{1,0:T(8,128)})) %all-reduce.43.cloned.1.call-update) | async-done | bytes 262160 | tf_op jit(solution)/shard_map/pmax | solution.py:77
  201.4 45.6 %all-reduce.23.cloned.1.call-done = f32[128,256]{1,0:T(8,128)} async-done(((f32[128,256]{1,0:T(8,128)}), f32[128,256]{1,0:T(8,128)}) %all-reduce.23.cloned.1.call-update) | async-done | bytes 131088 | tf_op jit(solution)/shard_map/pmax | solution.py:78
  247.0 0.9 rsqrt_multiply_fusion.7
  248.0 35.9 %all-reduce.25.cloned.1.call-done = f32[128,256]{1,0:T(8,128)} async-done(((f32[128,256]{1,0:T(8,128)}), f32[128,256]{1,0:T(8,128)}) %all-reduce.25.cloned.1.call-update) | async-done | bytes 131088 | tf_op jit(solution)/shard_map/pmax | solution.py:79
  283.9 0.9 rsqrt_multiply_fusion.6
  284.9 17.5 %while.77 = (s32[]{:T(128)}, f32[128,256]{1,0:T(8,128)S(1)}, f32[128,256]{1,0:T(8,128)S(1)}, s32[]{:T(128)}, s32[48]{0:T(128)}, /*index=5*/s32[]{:T(128)}, f32[4...) while((s32[]{:T(128)}, f32[128,256]{1,0:T(8,128)S(1)}, ...), condition=%wide.region_25.26_spmd.clone.clone, body=%wide.region_20.25_spmd.clone.clone.sunk | while | flops 4194374 | bytes 3240531 | solution.py:71
  285.6 0.8 compare_select_fusion.19
  287.5 2.3 fusion.35
  291.4 0.8 compare_select_fusion.19
  293.3 2.3 fusion.35
  297.2 0.8 compare_select_fusion.19
  299.1 2.3 fusion.35
  303.2 34.9 %all-reduce.41.cloned.1.call-done = (f32[128,256]{1,0:T(8,128)}, f32[128,256]{1,0:T(8,128)}) async-done(((f32[128,256]{1,0:T(8,128)}, f32[128,256]{1,0:T(8,128)}), (f32[128,256]{1,0:T(8,128)}, f32[128,256]{1,0:T(8,128)})) %all-reduce.41.cloned.1.call-update) | async-done | bytes 262160 | tf_op jit(solution)/shard_map/pmax | solution.py:77
  338.8 45.6 %all-reduce.27.cloned.1.call-done = f32[128,256]{1,0:T(8,128)} async-done(((f32[128,256]{1,0:T(8,128)}), f32[128,256]{1,0:T(8,128)}) %all-reduce.27.cloned.1.call-update) | async-done | bytes 131088 | tf_op jit(solution)/shard_map/pmax | solution.py:78
  384.5 0.9 rsqrt_multiply_fusion.5
  385.4 36.1 %all-reduce.29.cloned.1.call-done = f32[128,256]{1,0:T(8,128)} async-done(((f32[128,256]{1,0:T(8,128)}), f32[128,256]{1,0:T(8,128)}) %all-reduce.29.cloned.1.call-update) | async-done | bytes 131088 | tf_op jit(solution)/shard_map/pmax | solution.py:79
  421.5 0.9 rsqrt_multiply_fusion.4
  422.5 17.5 %while.78 = (s32[]{:T(128)}, f32[128,256]{1,0:T(8,128)S(1)}, f32[128,256]{1,0:T(8,128)S(1)}, s32[]{:T(128)}, s32[48]{0:T(128)}, /*index=5*/s32[]{:T(128)}, f32[4...) while((s32[]{:T(128)}, f32[128,256]{1,0:T(8,128)S(1)}, ...), condition=%wide.region_35.36_spmd.clone.clone, body=%wide.region_30.35_spmd.clone.clone.sunk | while | flops 4194374 | bytes 3240531 | solution.py:71
  423.1 0.8 compare_select_fusion.20
  425.0 2.3 fusion.36
  429.0 0.8 compare_select_fusion.20
  430.9 2.3 fusion.36
  434.8 0.8 compare_select_fusion.20
  436.7 2.3 fusion.36
  442.0 33.5 %all-reduce.39.cloned.1.call-done = (f32[128,256]{1,0:T(8,128)}, f32[128,256]{1,0:T(8,128)}) async-done(((f32[128,256]{1,0:T(8,128)}, f32[128,256]{1,0:T(8,128)}), (f32[128,256]{1,0:T(8,128)}, f32[128,256]{1,0:T(8,128)})) %all-reduce.39.cloned.1.call-update) | async-done | bytes 262160 | tf_op jit(solution)/shard_map/pmax | solution.py:77
  476.2 45.8 %all-reduce.31.cloned.1.call-done = f32[128,256]{1,0:T(8,128)} async-done(((f32[128,256]{1,0:T(8,128)}), f32[128,256]{1,0:T(8,128)}) %all-reduce.31.cloned.1.call-update) | async-done | bytes 131088 | tf_op jit(solution)/shard_map/pmax | solution.py:78
  522.0 0.9 rsqrt_multiply_fusion.3
  522.9 35.9 %all-reduce.33.cloned.1.call-done = f32[128,256]{1,0:T(8,128)} async-done(((f32[128,256]{1,0:T(8,128)}), f32[128,256]{1,0:T(8,128)}) %all-reduce.33.cloned.1.call-update) | async-done | bytes 131088 | tf_op jit(solution)/shard_map/pmax | solution.py:79
  558.9 0.9 rsqrt_multiply_fusion.2
  559.9 16.1 %while.79 = (s32[]{:T(128)}, f32[128,256]{1,0:T(8,128)S(1)}, f32[128,256]{1,0:T(8,128)S(1)}, s32[]{:T(128)}, s32[48]{0:T(128)}, /*index=5*/s32[]{:T(128)}, f32[4...) while((s32[]{:T(128)}, f32[128,256]{1,0:T(8,128)S(1)}, ...), condition=%wide.region_43.44_spmd.clone.clone, body=%wide.region_40.43_spmd.clone.clone.sunk | while | flops 9502790 | bytes 2712147 | solution.py:71
  560.5 0.8 compare_select_fusion.21
  562.5 2.3 fusion.39
  565.9 0.8 compare_select_fusion.21
  567.8 2.3 fusion.39
  571.3 0.8 compare_select_fusion.21
  573.2 2.3 fusion.39
  577.3 68.2 %all-reduce.35.cloned.1.call-done = f32[128,256]{1,0:T(8,128)} async-done(((f32[128,256]{1,0:T(8,128)}), f32[128,256]{1,0:T(8,128)}) %all-reduce.35.cloned.1.call-update) | async-done | bytes 131088 | tf_op jit(solution)/shard_map/psum | solution.py:83
  645.5 0.9 rsqrt_multiply_fusion.1
  647.0 0.7 copy.7
  647.7 54.8 %all-reduce.37.cloned.1.call-done = f32[128,256]{1,0:T(8,128)} async-done(((f32[128,256]{1,0:T(8,128)}), f32[128,256]{1,0:T(8,128)}) %all-reduce.37.cloned.1.call-update) | async-done | bytes 131088 | tf_op jit(solution)/shard_map/psum | solution.py:84
  702.5 0.9 rsqrt_multiply_fusion
  704.1 0.7 copy.8
  704.8 10.7 %multiply_select_fusion = f32[1,1,48,256,256]{4,3,2,1,0:T(8,128)} fusion(f32[1,1,48,256,256]{4,3,2,1,0:T(8,128)} %bitcast.25, f32[48,256]{1,0:T(8,128)S(1)} %gather_fusion.11, f32[48,256]{1,0:T(8,128)S(1)} %gather_fusion.10, pred[48]{0:T(512)(128)(4,1)S(1)} %iota_compare_fusion.12), kind=kLoop, calls=%fused_computation.79 | loop fusion | flops 9437184 | bytes 25264176 | tf_op jit(solution)/shard_map/jit(_where)/select_n | solution.py:89
  (223 shorter events, 46.7 us)
Async XLA Ops:
  7.2 56.2 %all-reduce.45.cloned.1.call-start = ((), (), s32[]{:S(2)}) async-start(), calls=%async_computation.13 | async-start | bytes 524288 | tf_op jit(solution)/shard_map/pmax | solution.py:77
  25.5 0.7 copy-start
  25.5 0.7 copy-start.1
  26.2 75.4 %all-reduce.21.cloned.1.call-start = ((), (), s32[]{:S(2)}) async-start(), calls=%async_computation.1 | async-start | bytes 262144 | tf_op jit(solution)/shard_map/pmax | solution.py:79
  63.4 83.1 %all-reduce.19.cloned.1.call-start = ((), (), s32[]{:S(2)}) async-start(), calls=%async_computation | async-start | bytes 262144 | tf_op jit(solution)/shard_map/pmax | solution.py:78
  64.1 136.6 %all-reduce.43.cloned.1.call-start = ((), (), s32[]{:S(2)}) async-start(), calls=%async_computation.12 | async-start | bytes 524288 | tf_op jit(solution)/shard_map/pmax | solution.py:77
  147.5 99.5 %copy-start.11 = (f32[128,256]{1,0:T(8,128)S(1)}, f32[128,256]{1,0:T(8,128)}, u32[]{:S(2)}) copy-start(f32[128,256]{1,0:T(8,128)} %all-reduce.19.cloned.1.call-done) | copy-start | bytes 393220
  147.5 136.4 %copy-start.10 = (f32[128,256]{1,0:T(8,128)S(1)}, f32[128,256]{1,0:T(8,128)}, u32[]{:S(2)}) copy-start(f32[128,256]{1,0:T(8,128)} %all-reduce.21.cloned.1.call-done) | copy-start | bytes 393220
  165.0 0.7 copy-start.2
  165.1 0.7 copy-start.3
  165.8 81.3 %all-reduce.23.cloned.1.call-start = ((), (), s32[]{:S(2)}) async-start(), calls=%async_computation.2 | async-start | bytes 262144 | tf_op jit(solution)/shard_map/pmax | solution.py:78
  200.8 83.1 %all-reduce.25.cloned.1.call-start = ((), (), s32[]{:S(2)}) async-start(), calls=%async_computation.3 | async-start | bytes 262144 | tf_op jit(solution)/shard_map/pmax | solution.py:79
  201.3 136.7 %all-reduce.41.cloned.1.call-start = ((), (), s32[]{:S(2)}) async-start(), calls=%async_computation.11 | async-start | bytes 524288 | tf_op jit(solution)/shard_map/pmax | solution.py:77
  302.4 0.7 copy-start.4
  302.4 0.7 copy-start.5
  303.1 81.3 %all-reduce.27.cloned.1.call-start = ((), (), s32[]{:S(2)}) async-start(), calls=%async_computation.4 | async-start | bytes 262144 | tf_op jit(solution)/shard_map/pmax | solution.py:78
  338.0 83.4 %all-reduce.29.cloned.1.call-start = ((), (), s32[]{:S(2)}) async-start(), calls=%async_computation.5 | async-start | bytes 262144 | tf_op jit(solution)/shard_map/pmax | solution.py:79
  338.8 136.8 %all-reduce.39.cloned.1.call-start = ((), (), s32[]{:S(2)}) async-start(), calls=%async_computation.10 | async-start | bytes 524288 | tf_op jit(solution)/shard_map/pmax | solution.py:77
  439.9 0.7 copy-start.6
  439.9 0.7 copy-start.7
  440.7 81.4 %all-reduce.31.cloned.1.call-start = ((), (), s32[]{:S(2)}) async-start(), calls=%async_computation.6 | async-start | bytes 262144 | tf_op jit(solution)/shard_map/pmax | solution.py:78
  475.6 83.3 %all-reduce.33.cloned.1.call-start = ((), (), s32[]{:S(2)}) async-start(), calls=%async_computation.7 | async-start | bytes 262144 | tf_op jit(solution)/shard_map/pmax | solution.py:79
  476.2 169.3 %all-reduce.35.cloned.1.call-start = ((), (), s32[]{:S(2)}) async-start(), calls=%async_computation.8 | async-start | bytes 262144 | tf_op jit(solution)/shard_map/psum | solution.py:83
  576.0 0.7 copy-start.9
  576.0 0.7 copy-start.8
  576.7 125.8 %all-reduce.37.cloned.1.call-start = ((), (), s32[]{:S(2)}) async-start(), calls=%async_computation.9 | async-start | bytes 262144 | tf_op jit(solution)/shard_map/psum | solution.py:84
Sparse Core Ops, SparseCore 0:
  26.3 36.9 all-reduce.44
  65.7 35.8 all-reduce.20
  104.5 41.9 all-reduce.18
  165.9 34.8 all-reduce.42
  203.5 43.4 all-reduce.22
  249.2 34.6 all-reduce.24
  303.2 34.7 all-reduce.40
  340.9 43.4 all-reduce.26
  386.8 34.6 all-reduce.28
  440.8 34.7 all-reduce.38
  478.5 43.4 all-reduce.30
  524.2 34.6 all-reduce.32
  576.8 68.5 all-reduce.34
  648.2 54.2 all-reduce.36
where the time goes:
time: 724 us; the launch traced here: 722 us
  waiting for transfers between devices  593 us (82%)
  other arithmetic  88.1 us (12%)
  local copies, waits for them, and re-layouts  23.1 us (3%)
  between operations  14.9 us (2%)
    pmax x4, waiting for transfers between devices, shards(): row_peak = lax.pmax(row_pair, 'col')  181 us
    pmax x4, waiting for transfers between devices, shards(): col_peak = lax.pmax(col_pair, 'row')  145 us
    pmax x4, waiting for transfers between devices, shards(): row_pair, col_pair = lax.pmax((row_part, col_part), 'depth')  140 us
    psum x1, waiting for transfers between devices, shards(): row_mass = lax.psum(row_part, ('col', 'depth'))  68.2 us
    psum x1, waiting for transfers between devices, shards(): col_mass = lax.psum(col_part, ('row', 'depth'))  54.8 us
    reduce_max x12, other arithmetic, step_block(): magnitude.max(axis=1)[None]  28.1 us
  transfers between devices with their start and end apart: 14, of which 14 were waited for; matrix products, arithmetic and copies ran while one was open for 1% of the time, Pallas kernels for 0%

commit v1 on v0

--- a/solution.py
+++ b/solution.py
@@ -81,7 +81,7 @@
         col_factor = col_factor * lax.rsqrt(col_peak + EPS)
     row_part, col_part = partials(row_factor, col_factor, True)
     row_mass = lax.psum(row_part, ("col", "depth"))
-    col_mass = lax.psum(col_part, ("row", "depth"))
+    col_mass = jnp.sum(lax.all_gather(col_part, ("row", "depth")), axis=0)
     row_factor = row_factor * lax.rsqrt(row_mass + EPS)
     col_factor = col_factor * lax.rsqrt(col_mass + EPS)
     live_all = jnp.arange(slot_count, dtype=jnp.int32) < live_count

time: 724 us -> 691 us (0.954)
  waiting for transfers between devices: 593 us -> 560 us
    psum x1 -> x0, waiting for transfers between devices: 54.8 us -> none  [shards(): col_mass = lax.psum(col_part, ('row', 'depth'))]
    all_gather x0 -> x1, waiting for transfers between devices: none -> 21.4 us  [shards(): col_mass = jnp.sum(lax.all_gather(col_part, ('row', 'depth')), axis=0)]
where the time goes in v1:
time: 691 us; the launch traced here: 689 us
  waiting for transfers between devices  560 us (81%)
  other arithmetic  88.5 us (13%)
  local copies, waits for them, and re-layouts  23.1 us (3%)
  between operations  14.9 us (2%)
    pmax x4, waiting for transfers between devices, shards(): row_peak = lax.pmax(row_pair, 'col')  181 us
    pmax x4, waiting for transfers between devices, shards(): col_peak = lax.pmax(col_pair, 'row')  145 us
    pmax x4, waiting for transfers between devices, shards(): row_pair, col_pair = lax.pmax((row_part, col_part), 'depth')  142 us
    psum x1, waiting for transfers between devices, shards(): row_mass = lax.psum(row_part, ('col', 'depth'))  66.8 us
    reduce_max x12, other arithmetic, step_block(): magnitude.max(axis=1)[None]  28.1 us
    all_gather x1, waiting for transfers between devices, shards(): col_mass = jnp.sum(lax.all_gather(col_part, ('row', 'depth')), axis=0)  21.4 us
  transfers between devices with their start and end apart: 14, of which 14 were waited for; matrix products, arithmetic and copies ran while one was open for 1% of the time, Pallas kernels for 0%

profile of v1, /device:TPU:0, one launch (start us, length us, event | category | flops | bytes accessed | tf_op | source)
XLA Modules:
  0.0 689.1 jit_solution(12937153035157331872)
XLA Ops:
  7.9 17.5 %while.75 = (s32[]{:T(128)}, f32[128,256]{1,0:T(8,128)S(1)}, f32[128,256]{1,0:T(8,128)S(1)}, s32[]{:T(128)}, s32[48]{0:T(128)}, /*index=5*/s32[]{:T(128)}, f32[4...) while((s32[]{:T(128)}, f32[128,256]{1,0:T(8,128)S(1)}, ...), condition=%wide.region_5.6_spmd.clone.clone, body=%wide.region_0.5_spmd.clone.clone.sunk | while | flops 4194374 | bytes 3371599 | solution.py:71
  8.6 0.8 compare_select_fusion.17
  10.6 2.3 fusion.33
  14.4 0.8 compare_select_fusion.17
  16.4 2.3 fusion.33
  20.3 0.8 compare_select_fusion.17
  22.3 2.3 fusion.33
  26.2 37.1 %all-reduce.42.cloned.1.call-done = (f32[128,256]{1,0:T(8,128)}, f32[128,256]{1,0:T(8,128)}) async-done(((f32[128,256]{1,0:T(8,128)}, f32[128,256]{1,0:T(8,128)}), (f32[128,256]{1,0:T(8,128)}, f32[128,256]{1,0:T(8,128)})) %all-reduce.42.cloned.1.call-update) | async-done | bytes 262160 | tf_op jit(solution)/shard_map/pmax | solution.py:77
  63.4 0.7 all-reduce.18.cloned.1.call-update
  64.2 37.4 %all-reduce.20.cloned.1.call-done = f32[128,256]{1,0:T(8,128)} async-done(((f32[128,256]{1,0:T(8,128)}), f32[128,256]{1,0:T(8,128)}) %all-reduce.20.cloned.1.call-update) | async-done | bytes 131088 | tf_op jit(solution)/shard_map/pmax | solution.py:79
  101.6 0.9 add_rsqrt_fusion
  102.5 44.0 %all-reduce.18.cloned.1.call-done = f32[128,256]{1,0:T(8,128)} async-done(((f32[128,256]{1,0:T(8,128)}), f32[128,256]{1,0:T(8,128)}) %all-reduce.18.cloned.1.call-update) | async-done | bytes 131088 | tf_op jit(solution)/shard_map/pmax | solution.py:78
  146.5 0.9 add_rsqrt_fusion.1
  147.5 17.5 %while.76 = (s32[]{:T(128)}, f32[128,256]{1,0:T(8,128)S(1)}, f32[128,256]{1,0:T(8,128)S(1)}, s32[]{:T(128)}, s32[48]{0:T(128)}, /*index=5*/s32[]{:T(128)}, f32[4...) while((s32[]{:T(128)}, f32[128,256]{1,0:T(8,128)S(1)}, ...), condition=%wide.region_15.16_spmd.clone.clone, body=%wide.region_10.15_spmd.clone.clone.sunk | while | flops 4194374 | bytes 3240531 | solution.py:71
  147.5 0.7 add_compare_fusion.11
  148.3 0.8 compare_select_fusion.18
  150.2 2.3 fusion.34
  154.1 0.8 compare_select_fusion.18
  156.0 2.3 fusion.34
  159.9 0.8 compare_select_fusion.18
  161.8 2.3 fusion.34
  165.8 34.9 %all-reduce.40.cloned.1.call-done = (f32[128,256]{1,0:T(8,128)}, f32[128,256]{1,0:T(8,128)}) async-done(((f32[128,256]{1,0:T(8,128)}, f32[128,256]{1,0:T(8,128)}), (f32[128,256]{1,0:T(8,128)}, f32[128,256]{1,0:T(8,128)})) %all-reduce.40.cloned.1.call-update) | async-done | bytes 262160 | tf_op jit(solution)/shard_map/pmax | solution.py:77
  201.4 45.6 %all-reduce.22.cloned.1.call-done = f32[128,256]{1,0:T(8,128)} async-done(((f32[128,256]{1,0:T(8,128)}), f32[128,256]{1,0:T(8,128)}) %all-reduce.22.cloned.1.call-update) | async-done | bytes 131088 | tf_op jit(solution)/shard_map/pmax | solution.py:78
  247.0 0.9 rsqrt_multiply_fusion.7
  248.0 35.9 %all-reduce.24.cloned.1.call-done = f32[128,256]{1,0:T(8,128)} async-done(((f32[128,256]{1,0:T(8,128)}), f32[128,256]{1,0:T(8,128)}) %all-reduce.24.cloned.1.call-update) | async-done | bytes 131088 | tf_op jit(solution)/shard_map/pmax | solution.py:79
  283.9 0.9 rsqrt_multiply_fusion.6
  284.9 17.5 %while.77 = (s32[]{:T(128)}, f32[128,256]{1,0:T(8,128)S(1)}, f32[128,256]{1,0:T(8,128)S(1)}, s32[]{:T(128)}, s32[48]{0:T(128)}, /*index=5*/s32[]{:T(128)}, f32[4...) while((s32[]{:T(128)}, f32[128,256]{1,0:T(8,128)S(1)}, ...), condition=%wide.region_25.26_spmd.clone.clone, body=%wide.region_20.25_spmd.clone.clone.sunk | while | flops 4194374 | bytes 3240531 | solution.py:71
  285.6 0.8 compare_select_fusion.19
  287.5 2.3 fusion.35
  291.4 0.8 compare_select_fusion.19
  293.3 2.3 fusion.35
  297.2 0.8 compare_select_fusion.19
  299.1 2.3 fusion.35
  303.2 34.9 %all-reduce.38.cloned.1.call-done = (f32[128,256]{1,0:T(8,128)}, f32[128,256]{1,0:T(8,128)}) async-done(((f32[128,256]{1,0:T(8,128)}, f32[128,256]{1,0:T(8,128)}), (f32[128,256]{1,0:T(8,128)}, f32[128,256]{1,0:T(8,128)})) %all-reduce.38.cloned.1.call-update) | async-done | bytes 262160 | tf_op jit(solution)/shard_map/pmax | solution.py:77
  338.8 45.6 %all-reduce.26.cloned.1.call-done = f32[128,256]{1,0:T(8,128)} async-done(((f32[128,256]{1,0:T(8,128)}), f32[128,256]{1,0:T(8,128)}) %all-reduce.26.cloned.1.call-update) | async-done | bytes 131088 | tf_op jit(solution)/shard_map/pmax | solution.py:78
  384.5 0.9 rsqrt_multiply_fusion.5
  385.4 36.1 %all-reduce.28.cloned.1.call-done = f32[128,256]{1,0:T(8,128)} async-done(((f32[128,256]{1,0:T(8,128)}), f32[128,256]{1,0:T(8,128)}) %all-reduce.28.cloned.1.call-update) | async-done | bytes 131088 | tf_op jit(solution)/shard_map/pmax | solution.py:79
  421.5 0.9 rsqrt_multiply_fusion.4
  422.5 17.5 %while.78 = (s32[]{:T(128)}, f32[128,256]{1,0:T(8,128)S(1)}, f32[128,256]{1,0:T(8,128)S(1)}, s32[]{:T(128)}, s32[48]{0:T(128)}, /*index=5*/s32[]{:T(128)}, f32[4...) while((s32[]{:T(128)}, f32[128,256]{1,0:T(8,128)S(1)}, ...), condition=%wide.region_35.36_spmd.clone.clone, body=%wide.region_30.35_spmd.clone.clone.sunk | while | flops 4194374 | bytes 3240531 | solution.py:71
  423.1 0.8 compare_select_fusion.20
  425.0 2.3 fusion.36
  429.0 0.8 compare_select_fusion.20
  430.9 2.3 fusion.36
  434.8 0.8 compare_select_fusion.20
  436.7 2.3 fusion.36
  440.7 34.9 %all-reduce.36.cloned.1.call-done = (f32[128,256]{1,0:T(8,128)}, f32[128,256]{1,0:T(8,128)}) async-done(((f32[128,256]{1,0:T(8,128)}, f32[128,256]{1,0:T(8,128)}), (f32[128,256]{1,0:T(8,128)}, f32[128,256]{1,0:T(8,128)})) %all-reduce.36.cloned.1.call-update) | async-done | bytes 262160 | tf_op jit(solution)/shard_map/pmax | solution.py:77
  476.2 45.8 %all-reduce.30.cloned.1.call-done = f32[128,256]{1,0:T(8,128)} async-done(((f32[128,256]{1,0:T(8,128)}), f32[128,256]{1,0:T(8,128)}) %all-reduce.30.cloned.1.call-update) | async-done | bytes 131088 | tf_op jit(solution)/shard_map/pmax | solution.py:78
  522.0 0.9 rsqrt_multiply_fusion.3
  522.9 35.9 %all-reduce.32.cloned.1.call-done = f32[128,256]{1,0:T(8,128)} async-done(((f32[128,256]{1,0:T(8,128)}), f32[128,256]{1,0:T(8,128)}) %all-reduce.32.cloned.1.call-update) | async-done | bytes 131088 | tf_op jit(solution)/shard_map/pmax | solution.py:79
  558.9 0.9 rsqrt_multiply_fusion.2
  559.9 16.1 %while.79 = (s32[]{:T(128)}, f32[128,256]{1,0:T(8,128)S(1)}, f32[128,256]{1,0:T(8,128)S(1)}, s32[]{:T(128)}, s32[48]{0:T(128)}, /*index=5*/s32[]{:T(128)}, f32[4...) while((s32[]{:T(128)}, f32[128,256]{1,0:T(8,128)S(1)}, ...), condition=%wide.region_43.44_spmd.clone.clone, body=%wide.region_40.43_spmd.clone.clone.sunk | while | flops 9502790 | bytes 2712147 | solution.py:71
  560.5 0.8 compare_select_fusion.21
  562.5 2.3 fusion.39
  565.9 0.8 compare_select_fusion.21
  567.8 2.3 fusion.39
  571.3 0.8 compare_select_fusion.21
  573.2 2.3 fusion.39
  578.6 66.8 %all-reduce.34.cloned.1.call-done = f32[128,256]{1,0:T(8,128)} async-done(((f32[128,256]{1,0:T(8,128)}), f32[128,256]{1,0:T(8,128)}) %all-reduce.34.cloned.1.call-update) | async-done | bytes 131088 | tf_op jit(solution)/shard_map/psum | solution.py:83
  645.5 0.9 rsqrt_multiply_fusion.1
  647.0 0.7 copy.7
  647.7 21.4 %all-gather.3.cloned.1.call-done = f32[1024,256]{1,0:T(8,128)} async-done(((f32[128,256]{1,0:T(8,128)}), f32[1024,256]{1,0:T(8,128)}) %all-gather.3.cloned.1.call-update) | async-done | bytes 1048592 | tf_op jit(solution)/shard_map/all_gather | solution.py:84
  669.2 1.3 reduce_sum.29
  671.1 0.7 copy.8
  671.8 10.7 %multiply_select_fusion = f32[1,1,48,256,256]{4,3,2,1,0:T(8,128)} fusion(f32[1,1,48,256,256]{4,3,2,1,0:T(8,128)} %bitcast.26, f32[48,256]{1,0:T(8,128)S(1)} %gather_fusion.11, f32[48,256]{1,0:T(8,128)S(1)} %gather_fusion.10, pred[48]{0:T(512)(128)(4,1)S(1)} %iota_compare_fusion.12), kind=kLoop, calls=%fused_computation.79 | loop fusion | flops 9437184 | bytes 25264176 | tf_op jit(solution)/shard_map/jit(_where)/select_n | solution.py:89
  (224 shorter events, 46.8 us)
Async XLA Ops:
  7.2 56.2 %all-reduce.42.cloned.1.call-start = ((), (), s32[]{:S(2)}) async-start(), calls=%async_computation.13 | async-start | bytes 524288 | tf_op jit(solution)/shard_map/pmax | solution.py:77
  25.5 0.7 copy-start
  25.5 0.7 copy-start.1
  26.2 75.4 %all-reduce.20.cloned.1.call-start = ((), (), s32[]{:S(2)}) async-start(), calls=%async_computation.1 | async-start | bytes 262144 | tf_op jit(solution)/shard_map/pmax | solution.py:79
  63.4 83.1 %all-reduce.18.cloned.1.call-start = ((), (), s32[]{:S(2)}) async-start(), calls=%async_computation | async-start | bytes 262144 | tf_op jit(solution)/shard_map/pmax | solution.py:78
  64.1 136.6 %all-reduce.40.cloned.1.call-start = ((), (), s32[]{:S(2)}) async-start(), calls=%async_computation.12 | async-start | bytes 524288 | tf_op jit(solution)/shard_map/pmax | solution.py:77
  147.5 99.5 %copy-start.11 = (f32[128,256]{1,0:T(8,128)S(1)}, f32[128,256]{1,0:T(8,128)}, u32[]{:S(2)}) copy-start(f32[128,256]{1,0:T(8,128)} %all-reduce.18.cloned.1.call-done) | copy-start | bytes 393220
  147.5 136.4 %copy-start.10 = (f32[128,256]{1,0:T(8,128)S(1)}, f32[128,256]{1,0:T(8,128)}, u32[]{:S(2)}) copy-start(f32[128,256]{1,0:T(8,128)} %all-reduce.20.cloned.1.call-done) | copy-start | bytes 393220
  165.0 0.7 copy-start.2
  165.1 0.7 copy-start.3
  165.8 81.3 %all-reduce.22.cloned.1.call-start = ((), (), s32[]{:S(2)}) async-start(), calls=%async_computation.2 | async-start | bytes 262144 | tf_op jit(solution)/shard_map/pmax | solution.py:78
  200.8 83.1 %all-reduce.24.cloned.1.call-start = ((), (), s32[]{:S(2)}) async-start(), calls=%async_computation.3 | async-start | bytes 262144 | tf_op jit(solution)/shard_map/pmax | solution.py:79
  201.3 136.7 %all-reduce.38.cloned.1.call-start = ((), (), s32[]{:S(2)}) async-start(), calls=%async_computation.11 | async-start | bytes 524288 | tf_op jit(solution)/shard_map/pmax | solution.py:77
  302.4 0.7 copy-start.4
  302.4 0.7 copy-start.5
  303.1 81.3 %all-reduce.26.cloned.1.call-start = ((), (), s32[]{:S(2)}) async-start(), calls=%async_computation.4 | async-start | bytes 262144 | tf_op jit(solution)/shard_map/pmax | solution.py:78
  338.0 83.4 %all-reduce.28.cloned.1.call-start = ((), (), s32[]{:S(2)}) async-start(), calls=%async_computation.5 | async-start | bytes 262144 | tf_op jit(solution)/shard_map/pmax | solution.py:79
  338.8 136.8 %all-reduce.36.cloned.1.call-start = ((), (), s32[]{:S(2)}) async-start(), calls=%async_computation.10 | async-start | bytes 524288 | tf_op jit(solution)/shard_map/pmax | solution.py:77
  439.9 0.7 copy-start.6
  439.9 0.7 copy-start.7
  440.7 81.4 %all-reduce.30.cloned.1.call-start = ((), (), s32[]{:S(2)}) async-start(), calls=%async_computation.6 | async-start | bytes 262144 | tf_op jit(solution)/shard_map/pmax | solution.py:78
  475.6 83.3 %all-reduce.32.cloned.1.call-start = ((), (), s32[]{:S(2)}) async-start(), calls=%async_computation.7 | async-start | bytes 262144 | tf_op jit(solution)/shard_map/pmax | solution.py:79
  476.2 169.3 %all-reduce.34.cloned.1.call-start = ((), (), s32[]{:S(2)}) async-start(), calls=%async_computation.8 | async-start | bytes 262144 | tf_op jit(solution)/shard_map/psum | solution.py:83
  576.0 0.7 copy-start.9
  576.0 0.7 copy-start.8
  576.7 92.5 %all-gather.3.cloned.1.call-start = ((), (), s32[]{:S(2)}) async-start(), calls=%async_computation.9 | async-start | bytes 1179648 | tf_op jit(solution)/shard_map/all_gather | solution.py:84
Sparse Core Ops, SparseCore 0:
  26.3 36.9 all-reduce.41
  65.7 35.8 all-reduce.19
  104.5 41.9 all-reduce.17
  165.9 34.8 all-reduce.39
  203.5 43.4 all-reduce.21
  249.2 34.6 all-reduce.23
  303.2 34.7 all-reduce.37
  340.9 43.4 all-reduce.25
  386.8 34.6 all-reduce.27
  440.8 34.7 all-reduce.35
  478.5 43.4 all-reduce.29
  524.2 34.6 all-reduce.31
  576.8 68.5 all-reduce.33
  647.5 21.6 all-gather.2
